TPU v7x, 32 devices: a whole 2x2x4 slice. The times are simulated.
32 devices in a mesh: rows: 8 (over z, x), grp: 4 (over y, core).
Axes of the slice: x: 2, y: 2, z: 4, core: 2. Of those that a mesh axis runs over, the one named last changes fastest.
Arguments:
- matrix: float32 [65536, 1024], P(('rows', 'grp'))
- row_signs: int32 [65536], P(('rows', 'grp')), may hold values from -1 to 1, as said below
- samples: int32 [8192], P(('rows', 'grp')), may hold values from 0 to 65535, as said below
Outputs:
- factor: float32 [1024, 1024], P('rows')
Inputs may be any that keep to these rules, and one draw needn't show every extreme that they name: `row_signs`: every entry is 1 or -1. `samples`: entries are distinct and increasing; entries k * 256 to (k + 1) * 256 - 1 lie in rows k * 2048 to (k + 1) * 2048 - 1.
All inputs are finite; a program needn't handle non-finite values.
Results may differ from a plain program's by a relative error of at most 0.00011.
Values sent between devices are 32-bit elements; how exact they have to be, the bound alone decides.
A program may use at most 128 MiB of HBM per device.

v0:
```python
import jax
import jax.numpy as jnp
from jax import lax
from jax.sharding import PartitionSpec as P

exact_mode = lax.Precision.HIGHEST


def parity_sign(left, right, length):
    correlation = left & right
    ones_total = jnp.zeros_like(correlation)
    for bit_level in range(max(1, length.bit_length() - 1)):
        ones_total = ones_total + (correlation >> bit_level & 1)
    return (1 - 2 * (ones_total % 2)).astype(jnp.float32)


def sylvester(length):
    indices = jnp.arange(length, dtype=jnp.int32)
    return parity_sign(indices[:, None], indices[None, :], length)


def shards(matrix, row_signs, samples):
    count_rows = lax.axis_size("rows")
    count_grp = lax.axis_size("grp")
    blocks = count_rows * count_grp
    row_dev, col_count = matrix.shape
    piece_rows = row_dev // blocks
    total_rows = row_dev * blocks
    sample_dev = samples.shape[0]
    position = lax.axis_index(("rows", "grp"))
    signed = matrix * row_signs.astype(jnp.float32)[:, None]
    before = jnp.dot(sylvester(row_dev), signed, precision=exact_mode)
    arrived = lax.all_to_all(
        lax.all_to_all(
            before.reshape(1, 1, row_dev, col_count),
            "rows",
            split_axis=2,
            concat_axis=0,
            tiled=True,
        ),
        "grp",
        split_axis=2,
        concat_axis=1,
        tiled=True,
    )
    mixed_rows = jnp.dot(
        sylvester(blocks), arrived.reshape(blocks, piece_rows * col_count), precision=exact_mode
    )
    mixed_rows = mixed_rows.reshape(count_rows, count_grp, piece_rows, col_count)
    mixed_rows = mixed_rows / jnp.sqrt(jnp.float32(total_rows))
    all_indices = lax.all_gather(samples, ("rows", "grp"), axis=0, tiled=True)
    owner_block = all_indices // row_dev
    within = all_indices % row_dev - position * piece_rows
    owner_hit = (owner_block[:, None] == jnp.arange(blocks, dtype=jnp.int32)[None, :]).astype(
        jnp.float32
    )
    local_hit = (within[:, None] == jnp.arange(piece_rows, dtype=jnp.int32)[None, :]).astype(
        jnp.float32
    )
    weights = jnp.einsum("kb,kt->bt", owner_hit, local_hit, precision=exact_mode).reshape(
        blocks * piece_rows
    )
    flat_rows = mixed_rows.reshape(blocks * piece_rows, col_count)
    local_gram = jnp.einsum(
        "kn,km->nm", flat_rows * weights[:, None], flat_rows, precision=exact_mode
    )
    summed_gram = lax.psum(local_gram, ("rows", "grp"))
    gram_total = summed_gram * (total_rows / (sample_dev * blocks))
    lower_factor = jnp.linalg.cholesky(gram_total)
    upper_factor = lower_factor.T
    share_rows = col_count // count_rows
    return lax.dynamic_slice_in_dim(
        upper_factor, lax.axis_index("rows") * share_rows, share_rows, 0
    )


def solution(mesh):
    return jax.shard_map(
        shards,
        mesh=mesh,
        in_specs=(P(("rows", "grp"), None), P(("rows", "grp")), P(("rows", "grp"))),
        out_specs=P("rows", None),
        check_vma=False,
    )
```

profile of v0, /device:TPU:0, one launch (start us, length us, event | category | flops | bytes accessed | tf_op | source)
XLA Modules:
  0.0 873.1 jit_solution(1184886997414699403)
XLA Ops:
  6.5 0.7 convert_element_type.30
  7.2 4.0 fusion.115
  11.2 93.9 %fusion.26 = f32[1,1,2048,1024]{3,2,1,0:T(8,128)S(1)} fusion(f32[2048,1024]{1,0:T(8,128)S(1)} %fusion.115), kind=kOutput, calls=%fused_computation.29 | convolution fusion | flops 51736739840 | bytes 16777216 | tf_op jit(solution)/shard_map/dot_general | solution.py:32
  105.2 10.7 %copy.40 = f32[1,1,2048,1024]{3,1,0,2:T(1,128)S(1)} copy(f32[1,1,2048,1024]{3,2,1,0:T(8,128)S(1)} %fusion.26) | data formatting | bytes 16777216 | tf_op jit(solution)/shard_map/reshape | solution.py:35
  115.9 190.1 %all_to_all.21 = f32[1,1,2048,1024]{3,1,0,2:T(1,128)S(1)} all-to-all(f32[1,1,2048,1024]{3,1,0,2:T(1,128)S(1)} %copy.40), channel_id=1, replica_groups=mesh['rows'=8,'grp'=4] {'rows'}, dimensions={2} | all-to-all | bytes 16777216 | tf_op jit(solution)/shard_map/all_to_all | solution.py:34
  306.0 8.1 copy.41
  314.1 5.8 all-to-all-start.1
  320.0 123.8 %all-gather = s32[32,1,256]{2,1,0:T(1,128)S(1)} all-gather(s32[1,1,256]{2,1,0:T(1,128)S(1)} %bitcast.77), channel_id=1, replica_groups=mesh['rows'=8,'grp'=4] {'rows','grp'}, dimensions={0}, use_global_device_ids=true | all-gather | bytes 33792 | tf_op jit(solution)/shard_map/all_gather | solution.py:51
  443.8 0.6 fusion.41
  444.5 11.4 %copy.42 = f32[8,1,256,1024]{3,2,0,1:T(8,128)} copy(f32[8,1,256,1024]{3,0,1,2:T(8,128)} %all-to-all-done.1) | data formatting | bytes 16777216 | tf_op jit(solution)/shard_map/all_to_all | solution.py:33
  456.0 7.5 reshape.191
  463.4 10.6 %fusion.9 = f32[8,4,64,1024]{3,0,2,1:T(8,128)S(1)} fusion(f32[4,64,8,1024]{3,2,1,0:T(8,128)} %bitcast.73, s32[8,4]{0,1:T(4,128)S(1)} %multiply_add_fusion), kind=kOutput, calls=%fused_computation.12 | convolution fusion | flops 805336064 | bytes 16777344 | tf_op jit(solution)/shard_map/dot_general | solution.py:46
  474.1 31.2 %fusion.35 = f32[1024,1024]{0,1:T(8,128)} fusion(f32[8,4,64,1024]{3,0,2,1:T(8,128)S(1)} %fusion.9, f32[8,4,64]{0,2,1:T(8,128)S(1)} %copy.44), kind=kOutput, calls=%fused_computation.35 | convolution fusion | flops 25773998080 | bytes 12591104 | tf_op jit(solution)/shard_map/kn,km->nm/dot_general | solution.py:64
  505.4 138.7 %all-reduce.3.cloned.1.call-done = f32[1024,1024]{0,1:T(8,128)} async-done(((f32[1024,1024]{0,1:T(8,128)}), f32[1024,1024]{0,1:T(8,128)}) %all-reduce.3.cloned.1.call-update) | async-done | bytes 4194320 | tf_op jit(solution)/shard_map/psum | solution.py:67
  644.0 5.0 broadcast_multiply_fusion
  649.0 5.3 copy.46
  654.4 4.4 fusion.31
  658.8 1.9 copy-done
  660.8 11.7 %cholesky.223 = f32[128,128]{1,0:T(8,128)S(1)} custom-call(f32[128,128]{1,0:T(8,128)S(1)} %cholesky.580), custom_call_target="Cholesky" | custom-call | tf_op jit(solution)/shard_map/jit(cholesky)/cholesky | solution.py:69
  672.5 2.5 cholesky.255
  675.0 9.8 %custom-call.59 = f32[1,128,128]{1,2,0:T(8,128)S(1)} custom-call(f32[1,128,128]{2,1,0:T(8,128)S(1)} %get-tuple-element.26), custom_call_target="InvertDiagBlocksLowerTriangular" | custom-call | tf_op jit(solution)/shard_map/jit(cholesky)/cholesky | solution.py:69
  684.8 2.4 constant_dynamic-update-slice_fusion.7
  687.2 1.5 convolution_subtract_fusion
  688.8 12.1 %cholesky.244 = f32[128,128]{1,0:T(8,128)S(1)} custom-call(f32[128,128]{1,0:T(8,128)S(1)} %cholesky.584), custom_call_target="Cholesky" | custom-call | tf_op jit(solution)/shard_map/jit(cholesky)/cholesky | solution.py:69
  700.8 0.6 select_reduce_fusion.6
  701.5 9.8 %custom-call.60 = f32[1,128,128]{1,2,0:T(8,128)S(1)} custom-call(f32[1,128,128]{2,1,0:T(8,128)S(1)} %get-tuple-element.23), custom_call_target="InvertDiagBlocksLowerTriangular" | custom-call | tf_op jit(solution)/shard_map/jit(cholesky)/cholesky | solution.py:69
  711.3 1.2 convolution_dynamic-update-slice_fusion
  712.6 2.1 convolution_subtract_fusion.1
  714.7 11.7 %cholesky.468 = f32[128,128]{1,0:T(8,128)S(1)} custom-call(f32[128,128]{1,0:T(8,128)S(1)} %cholesky.589), custom_call_target="Cholesky" | custom-call | tf_op jit(solution)/shard_map/jit(cholesky)/cholesky | solution.py:69
  726.4 0.6 select_reduce_fusion.5
  727.0 9.8 %custom-call.61 = f32[1,128,128]{1,2,0:T(8,128)S(1)} custom-call(f32[1,128,128]{2,1,0:T(8,128)S(1)} %get-tuple-element.20), custom_call_target="InvertDiagBlocksLowerTriangular" | custom-call | tf_op jit(solution)/shard_map/jit(cholesky)/cholesky | solution.py:69
  736.8 1.2 convolution_dynamic-update-slice_fusion.1
  738.0 2.3 convolution_subtract_fusion.2
  740.3 11.9 %cholesky.487 = f32[128,128]{1,0:T(8,128)S(1)} custom-call(f32[128,128]{1,0:T(8,128)S(1)} %cholesky.594), custom_call_target="Cholesky" | custom-call | tf_op jit(solution)/shard_map/jit(cholesky)/cholesky | solution.py:69
  752.2 0.6 select_reduce_fusion.4
  752.9 9.8 %custom-call.62 = f32[1,128,128]{1,2,0:T(8,128)S(1)} custom-call(f32[1,128,128]{2,1,0:T(8,128)S(1)} %get-tuple-element.17), custom_call_target="InvertDiagBlocksLowerTriangular" | custom-call | tf_op jit(solution)/shard_map/jit(cholesky)/cholesky | solution.py:69
  762.7 1.1 convolution_dynamic-update-slice_fusion.2
  763.8 2.3 convolution_subtract_fusion.3
  766.1 11.7 %cholesky.506 = f32[128,128]{1,0:T(8,128)S(1)} custom-call(f32[128,128]{1,0:T(8,128)S(1)} %cholesky.599), custom_call_target="Cholesky" | custom-call | tf_op jit(solution)/shard_map/jit(cholesky)/cholesky | solution.py:69
  777.8 0.6 select_reduce_fusion.3
  778.5 10.0 %custom-call.63 = f32[1,128,128]{1,2,0:T(8,128)S(1)} custom-call(f32[1,128,128]{2,1,0:T(8,128)S(1)} %get-tuple-element.14), custom_call_target="InvertDiagBlocksLowerTriangular" | custom-call | tf_op jit(solution)/shard_map/jit(cholesky)/cholesky | solution.py:69
  788.5 1.0 convolution_dynamic-update-slice_fusion.3
  789.5 2.3 convolution_subtract_fusion.4
  791.8 11.7 %cholesky.526 = f32[128,128]{1,0:T(8,128)S(1)} custom-call(f32[128,128]{1,0:T(8,128)S(1)} %cholesky.604), custom_call_target="Cholesky" | custom-call | tf_op jit(solution)/shard_map/jit(cholesky)/cholesky | solution.py:69
  803.5 0.6 select_reduce_fusion.2
  804.2 9.8 %custom-call.64 = f32[1,128,128]{1,2,0:T(8,128)S(1)} custom-call(f32[1,128,128]{2,1,0:T(8,128)S(1)} %get-tuple-element.11), custom_call_target="InvertDiagBlocksLowerTriangular" | custom-call | tf_op jit(solution)/shard_map/jit(cholesky)/cholesky | solution.py:69
  814.0 0.9 convolution_dynamic-update-slice_fusion.4
  814.9 2.0 convolution_subtract_fusion.5
  817.0 11.7 %cholesky.546 = f32[128,128]{1,0:T(8,128)S(1)} custom-call(f32[128,128]{1,0:T(8,128)S(1)} %cholesky.609), custom_call_target="Cholesky" | custom-call | tf_op jit(solution)/shard_map/jit(cholesky)/cholesky | solution.py:69
  828.7 0.6 select_reduce_fusion.1
  829.3 9.8 %custom-call.65 = f32[1,128,128]{1,2,0:T(8,128)S(1)} custom-call(f32[1,128,128]{2,1,0:T(8,128)S(1)} %get-tuple-element.8), custom_call_target="InvertDiagBlocksLowerTriangular" | custom-call | tf_op jit(solution)/shard_map/jit(cholesky)/cholesky | solution.py:69
  839.2 0.8 convolution_dynamic-update-slice_fusion.5
  840.0 1.8 convolution_subtract_fusion.6
  841.8 11.7 %cholesky.564 = f32[128,128]{1,0:T(8,128)S(1)} custom-call(f32[128,128]{1,0:T(8,128)S(1)} %convolution_subtract_fusion.6), custom_call_target="Cholesky" | custom-call | tf_op jit(solution)/shard_map/jit(cholesky)/cholesky | solution.py:69
  853.5 0.6 select_reduce_fusion
  854.1 0.7 compare_reduce_fusion.5
  854.8 0.6 compare_reduce_fusion.4
  855.5 0.7 compare_reduce_fusion.3
  856.1 0.7 compare_reduce_fusion.2
  856.8 0.7 compare_reduce_fusion.1
  857.5 0.6 compare_reduce_fusion
  858.1 0.6 compare_reduce_fusion.6
  863.7 1.1 fusion.49
  864.8 1.0 copy.47
  (17 shorter events, 0.3 us)
Async XLA Ops:
  314.1 5.9 copy-start.1
  314.1 130.4 %all-to-all-start.1 = ((f32[8,1,256,1024]{3,0,1,2:T(8,128)}), f32[8,1,256,1024]{3,0,1,2:T(8,128)}, u32[]{:S(2)}, u32[]{:S(2)}) async-start(f32[8,1,256,1024]{3,0,1,2:T(8,128)} %copy.41), calls=%async_computation.1 | async-start | bytes 16777216 | tf_op jit(solution)/shard_map/all_to_all | solution.py:33
  319.9 324.1 %all-reduce.3.cloned.1.call-start = ((), (), s32[]{:S(2)}) async-start(), calls=%async_computation.2 | async-start | bytes 8388608 | tf_op jit(solution)/shard_map/psum | solution.py:67
  658.8 1.9 copy-start
Sparse Core Ops, SparseCore 0:
  505.5 138.4 all-reduce.2
where the time goes:
time: 885 us; the launch traced here: 873 us
  blocking collectives  314 us (35%)
  other arithmetic  188 us (21%)
  matrix products  159 us (18%)
  waiting for transfers between devices  139 us (16%)
  local copies, waits for them, and re-layouts  48.6 us (5%)
  between operations  19.1 us (2%)
    all_to_all x1, blocking collectives, shards(): lax.all_to_all(before.reshape(1, 1, row_dev, col_count), 'rows', split_ax...  190 us
    another operation x30, other arithmetic, shards(): lower_factor = jnp.linalg.cholesky(gram_total)  172 us
    psum x1, waiting for transfers between devices, shards(): summed_gram = lax.psum(local_gram, ('rows', 'grp'))  139 us
    all_gather x1, blocking collectives, shards(): all_indices = lax.all_gather(samples, ('rows', 'grp'), axis=0, tiled=True)  124 us
    dot_general x1, matrix products, shards(): before = jnp.dot(sylvester(row_dev), signed, precision=exact_mode)  93.9 us
    dot_general x1, matrix products, shards(): jnp.einsum('kn,km->nm', flat_rows * weights[:, None], flat_rows, precisio...  31.2 us
    another operation x14, matrix products, shards(): lower_factor = jnp.linalg.cholesky(gram_total)  23.1 us
  transfers between devices with their start and end apart: 2, of which 1 were waited for; matrix products, arithmetic and copies ran while one was open for 0% of the time, Pallas kernels for 0%

commit v1 on v0

--- a/solution.py
+++ b/solution.py
@@ -4,6 +4,15 @@
 from jax.sharding import PartitionSpec as P
 
 exact_mode = lax.Precision.HIGHEST
+
+
+def list_fields(point):
+    return jnp.concatenate(
+        jax.lax.all_to_all(
+            jnp.stack(jnp.split(point, jax.lax.axis_size("rows"), axis=2), 0), "rows", 0, 0
+        ),
+        0,
+    )
 
 
 def parity_sign(left, right, length):
@@ -31,13 +40,7 @@
     signed = matrix * row_signs.astype(jnp.float32)[:, None]
     before = jnp.dot(sylvester(row_dev), signed, precision=exact_mode)
     arrived = lax.all_to_all(
-        lax.all_to_all(
-            before.reshape(1, 1, row_dev, col_count),
-            "rows",
-            split_axis=2,
-            concat_axis=0,
-            tiled=True,
-        ),
+        list_fields(before.reshape(1, 1, row_dev, col_count)),
         "grp",
         split_axis=2,
         concat_axis=1,

time: 885 us -> 875 us (0.989)
  local copies, waits for them, and re-layouts: 48.6 us -> 38.5 us
    all_to_all x2 -> x1, local copies, waits for them, and re-layouts: 19.5 us -> 11.4 us  [shards(): lax.all_to_all(list_fields(before.reshape(1, 1, row_dev, col_count)), 'gr...]
where the time goes in v1:
time: 875 us; the launch traced here: 863 us
  blocking collectives  314 us (36%)
  other arithmetic  188 us (21%)
  matrix products  160 us (18%)
  waiting for transfers between devices  139 us (16%)
  local copies, waits for them, and re-layouts  38.5 us (4%)
  between operations  19 us (2%)
    all_to_all x1, blocking collectives, list_fields(): jax.lax.all_to_all(jnp.stack(jnp.split(point, jax.lax.axis_size('rows'),...  190 us
    another operation x30, other arithmetic, shards(): lower_factor = jnp.linalg.cholesky(gram_total)  172 us
    psum x1, waiting for transfers between devices, shards(): summed_gram = lax.psum(local_gram, ('rows', 'grp'))  139 us
    all_gather x1, blocking collectives, shards(): all_indices = lax.all_gather(samples, ('rows', 'grp'), axis=0, tiled=True)  124 us
    dot_general x1, matrix products, shards(): before = jnp.dot(sylvester(row_dev), signed, precision=exact_mode)  94.3 us
    dot_general x1, matrix products, shards(): jnp.einsum('kn,km->nm', flat_rows * weights[:, None], flat_rows, precisio...  31.2 us
    another operation x14, matrix products, shards(): lower_factor = jnp.linalg.cholesky(gram_total)  23.1 us
  transfers between devices with their start and end apart: 2, of which 1 were waited for; matrix products, arithmetic and copies ran while one was open for 0% of the time, Pallas kernels for 0%

profile of v1, /device:TPU:0, one launch (start us, length us, event | category | flops | bytes accessed | tf_op | source)
XLA Modules:
  0.0 863.2 jit_solution(403141761070589356)
XLA Ops:
  6.5 0.7 convert_element_type.30
  7.2 4.0 fusion.123
  11.2 94.3 %fusion.26 = f32[1,1,2048,1024]{3,2,1,0:T(8,128)S(1)} fusion(f32[2048,1024]{1,0:T(8,128)S(1)} %fusion.123), kind=kOutput, calls=%fused_computation.29 | convolution fusion | flops 51736739840 | bytes 16777216 | tf_op jit(solution)/shard_map/dot_general | solution.py:41
  106.1 190.1 %all_to_all.14 = f32[8,1,1,256,1024]{4,3,2,1,0:T(8,128)S(1)} all-to-all(f32[8,1,1,256,1024]{4,3,2,1,0:T(8,128)S(1)} %fusion.43), channel_id=1, replica_groups=mesh['rows'=8,'grp'=4] {'rows'}, dimensions={0} | all-to-all | bytes 16777216 | tf_op jit(solution)/shard_map/all_to_all | solution.py:11
  296.3 8.1 copy.37
  304.3 5.8 all-to-all-start.1
  310.2 123.8 %all-gather = s32[32,1,256]{2,1,0:T(1,128)S(1)} all-gather(s32[1,1,256]{2,1,0:T(1,128)S(1)} %bitcast.109), channel_id=1, replica_groups=mesh['rows'=8,'grp'=4] {'rows','grp'}, dimensions={0}, use_global_device_ids=true | all-gather | bytes 33792 | tf_op jit(solution)/shard_map/all_gather | solution.py:54
  434.1 0.6 fusion.41
  434.6 0.1 copy.40
  434.8 11.4 %copy.38 = f32[8,1,256,1024]{3,2,0,1:T(8,128)} copy(f32[8,1,256,1024]{3,0,1,2:T(8,128)} %all-to-all-done.1) | data formatting | bytes 16777216 | tf_op jit(solution)/shard_map/all_to_all | solution.py:42
  446.2 7.5 reshape.192
  453.7 10.6 %fusion.9 = f32[8,4,64,1024]{3,0,2,1:T(8,128)S(1)} fusion(f32[4,64,8,1024]{3,2,1,0:T(8,128)} %bitcast.105, s32[8,4]{0,1:T(4,128)S(1)} %multiply_add_fusion), kind=kOutput, calls=%fused_computation.12 | convolution fusion | flops 805336064 | bytes 16777344 | tf_op jit(solution)/shard_map/dot_general | solution.py:49
  464.3 31.2 %fusion.35 = f32[1024,1024]{0,1:T(8,128)} fusion(f32[8,4,64,1024]{3,0,2,1:T(8,128)S(1)} %fusion.9, f32[8,4,64]{0,2,1:T(8,128)S(1)} %copy.40), kind=kOutput, calls=%fused_computation.35 | convolution fusion | flops 25773998080 | bytes 12591104 | tf_op jit(solution)/shard_map/kn,km->nm/dot_general | solution.py:67
  495.6 138.5 %all-reduce.3.cloned.1.call-done = f32[1024,1024]{0,1:T(8,128)} async-done(((f32[1024,1024]{0,1:T(8,128)}), f32[1024,1024]{0,1:T(8,128)}) %all-reduce.3.cloned.1.call-update) | async-done | bytes 4194320 | tf_op jit(solution)/shard_map/psum | solution.py:70
  634.1 5.0 broadcast_multiply_fusion
  639.1 5.3 copy.42
  644.4 4.4 fusion.31
  648.9 1.9 copy-done
  650.8 11.7 %cholesky.223 = f32[128,128]{1,0:T(8,128)S(1)} custom-call(f32[128,128]{1,0:T(8,128)S(1)} %cholesky.580), custom_call_target="Cholesky" | custom-call | tf_op jit(solution)/shard_map/jit(cholesky)/cholesky | solution.py:72
  662.6 9.8 %custom-call.59 = f32[1,128,128]{1,2,0:T(8,128)S(1)} custom-call(f32[1,128,128]{2,1,0:T(8,128)S(1)} %get-tuple-element.26), custom_call_target="InvertDiagBlocksLowerTriangular" | custom-call | tf_op jit(solution)/shard_map/jit(cholesky)/cholesky | solution.py:72
  672.4 2.5 cholesky.255
  674.9 2.4 constant_dynamic-update-slice_fusion.7
  677.3 1.5 convolution_subtract_fusion
  678.8 12.1 %cholesky.244 = f32[128,128]{1,0:T(8,128)S(1)} custom-call(f32[128,128]{1,0:T(8,128)S(1)} %cholesky.584), custom_call_target="Cholesky" | custom-call | tf_op jit(solution)/shard_map/jit(cholesky)/cholesky | solution.py:72
  690.9 0.6 select_reduce_fusion.6
  691.6 9.8 %custom-call.60 = f32[1,128,128]{1,2,0:T(8,128)S(1)} custom-call(f32[1,128,128]{2,1,0:T(8,128)S(1)} %get-tuple-element.23), custom_call_target="InvertDiagBlocksLowerTriangular" | custom-call | tf_op jit(solution)/shard_map/jit(cholesky)/cholesky | solution.py:72
  701.4 1.2 convolution_dynamic-update-slice_fusion
  702.6 2.1 convolution_subtract_fusion.1
  704.7 11.7 %cholesky.468 = f32[128,128]{1,0:T(8,128)S(1)} custom-call(f32[128,128]{1,0:T(8,128)S(1)} %cholesky.589), custom_call_target="Cholesky" | custom-call | tf_op jit(solution)/shard_map/jit(cholesky)/cholesky | solution.py:72
  716.4 0.6 select_reduce_fusion.5
  717.1 0.6 compare_reduce_fusion.5
  717.7 9.8 %custom-call.61 = f32[1,128,128]{1,2,0:T(8,128)S(1)} custom-call(f32[1,128,128]{2,1,0:T(8,128)S(1)} %get-tuple-element.20), custom_call_target="InvertDiagBlocksLowerTriangular" | custom-call | tf_op jit(solution)/shard_map/jit(cholesky)/cholesky | solution.py:72
  727.5 1.2 convolution_dynamic-update-slice_fusion.1
  728.7 2.3 convolution_subtract_fusion.2
  731.0 11.9 %cholesky.487 = f32[128,128]{1,0:T(8,128)S(1)} custom-call(f32[128,128]{1,0:T(8,128)S(1)} %cholesky.594), custom_call_target="Cholesky" | custom-call | tf_op jit(solution)/shard_map/jit(cholesky)/cholesky | solution.py:72
  742.9 0.6 select_reduce_fusion.4
  743.6 0.6 compare_reduce_fusion.4
  744.2 9.8 %custom-call.62 = f32[1,128,128]{1,2,0:T(8,128)S(1)} custom-call(f32[1,128,128]{2,1,0:T(8,128)S(1)} %get-tuple-element.17), custom_call_target="InvertDiagBlocksLowerTriangular" | custom-call | tf_op jit(solution)/shard_map/jit(cholesky)/cholesky | solution.py:72
  754.0 1.1 convolution_dynamic-update-slice_fusion.2
  755.1 2.3 convolution_subtract_fusion.3
  757.5 11.7 %cholesky.506 = f32[128,128]{1,0:T(8,128)S(1)} custom-call(f32[128,128]{1,0:T(8,128)S(1)} %cholesky.599), custom_call_target="Cholesky" | custom-call | tf_op jit(solution)/shard_map/jit(cholesky)/cholesky | solution.py:72
  769.2 0.6 select_reduce_fusion.3
  769.8 0.6 compare_reduce_fusion.3
  770.5 10.0 %custom-call.63 = f32[1,128,128]{1,2,0:T(8,128)S(1)} custom-call(f32[1,128,128]{2,1,0:T(8,128)S(1)} %get-tuple-element.14), custom_call_target="InvertDiagBlocksLowerTriangular" | custom-call | tf_op jit(solution)/shard_map/jit(cholesky)/cholesky | solution.py:72
  780.5 1.0 convolution_dynamic-update-slice_fusion.3
  781.5 2.3 convolution_subtract_fusion.4
  783.8 11.7 %cholesky.526 = f32[128,128]{1,0:T(8,128)S(1)} custom-call(f32[128,128]{1,0:T(8,128)S(1)} %cholesky.604), custom_call_target="Cholesky" | custom-call | tf_op jit(solution)/shard_map/jit(cholesky)/cholesky | solution.py:72
  795.5 0.6 select_reduce_fusion.2
  796.1 0.6 compare_reduce_fusion.2
  796.8 9.8 %custom-call.64 = f32[1,128,128]{1,2,0:T(8,128)S(1)} custom-call(f32[1,128,128]{2,1,0:T(8,128)S(1)} %get-tuple-element.11), custom_call_target="InvertDiagBlocksLowerTriangular" | custom-call | tf_op jit(solution)/shard_map/jit(cholesky)/cholesky | solution.py:72
  806.6 0.9 convolution_dynamic-update-slice_fusion.4
  807.5 2.0 convolution_subtract_fusion.5
  809.6 11.9 %cholesky.546 = f32[128,128]{1,0:T(8,128)S(1)} custom-call(f32[128,128]{1,0:T(8,128)S(1)} %cholesky.609), custom_call_target="Cholesky" | custom-call | tf_op jit(solution)/shard_map/jit(cholesky)/cholesky | solution.py:72
  821.5 0.6 select_reduce_fusion.1
  822.2 0.6 compare_reduce_fusion.1
  822.8 9.8 %custom-call.65 = f32[1,128,128]{1,2,0:T(8,128)S(1)} custom-call(f32[1,128,128]{2,1,0:T(8,128)S(1)} %get-tuple-element.8), custom_call_target="InvertDiagBlocksLowerTriangular" | custom-call | tf_op jit(solution)/shard_map/jit(cholesky)/cholesky | solution.py:72
  832.6 0.8 convolution_dynamic-update-slice_fusion.5
  833.4 1.8 convolution_subtract_fusion.6
  835.2 11.7 %cholesky.564 = f32[128,128]{1,0:T(8,128)S(1)} custom-call(f32[128,128]{1,0:T(8,128)S(1)} %convolution_subtract_fusion.6), custom_call_target="Cholesky" | custom-call | tf_op jit(solution)/shard_map/jit(cholesky)/cholesky | solution.py:72
  846.9 0.6 select_reduce_fusion
  847.6 0.7 compare_reduce_fusion
  848.3 0.6 compare_reduce_fusion.6
  853.8 1.1 fusion.57
  854.9 1.0 copy.43
  (24 shorter events, 0.8 us)
Async XLA Ops:
  304.3 5.9 copy-start.1
  304.3 130.4 %all-to-all-start.1 = ((f32[8,1,256,1024]{3,0,1,2:T(8,128)}), f32[8,1,256,1024]{3,0,1,2:T(8,128)}, u32[]{:S(2)}, u32[]{:S(2)}) async-start(f32[8,1,256,1024]{3,0,1,2:T(8,128)} %copy.37), calls=%async_computation.1 | async-start | bytes 16777216 | tf_op jit(solution)/shard_map/all_to_all | solution.py:42
  310.1 324.0 %all-reduce.3.cloned.1.call-start = ((), (), s32[]{:S(2)}) async-start(), calls=%async_computation.2 | async-start | bytes 8388608 | tf_op jit(solution)/shard_map/psum | solution.py:70
  648.9 1.9 copy-start
Sparse Core Ops, SparseCore 0:
  495.7 138.3 all-reduce.2
